TPU v7x, 256 devices: a whole 4x4x8 slice. The times are simulated.
256 devices in a mesh: seq: 32 (over z, x), head: 8 (over y, core).
Axes of the slice: x: 4, y: 4, z: 8, core: 2. Of those that a mesh axis runs over, the one named last changes fastest.
Arguments:
- corpus: bfloat16 [128, 128, 4096], P('seq'), may hold values from -8 to 8
- enc_qkv: bfloat16 [4096, 16, 3, 128], P(None, 'head'), may hold values from -0.1015625 to 0.1015625
- enc_out: bfloat16 [16, 128, 4096], P('head'), may hold values from -0.375 to 0.375
- cca_kv: bfloat16 [4096, 16, 2, 128], P('seq', 'head'), may hold values from -0.09375 to 0.09375
- gain_in: float32 [4096], replicated, may hold values from 0.5 to 2
- gain_out: float32 [4096], replicated, may hold values from 0.5 to 2
- queries: bfloat16 [16384, 16, 128], P('seq', 'head'), may hold values from -100 to 100
- nbr_ids: int32 [256, 2], P('seq'), may hold values from 0 to 127, as said below
Outputs:
- cca_out: bfloat16 [16384, 16, 128], P('seq', 'head')
Inputs may be any that keep to these rules, and one draw needn't show every extreme that they name: `nbr_ids`: entry [u, n] is the corpus row of group u's n-th neighbour; row r is held by index r // 4 of seq. The neighbours of one group differ. Among the requests of the 8 groups of one index of seq no owner is named more than 2 times, and in every draw some owner is named exactly 2 times by every index of seq.
All inputs are finite; a program needn't handle non-finite values.
Results may differ from a plain program's by a relative error of at most 0.03.
Values may be sent and summed in bfloat16 or wider, within the bound.
No kernel may reach another device: no remote copies, remote signals or barrier semaphores. Data moves between devices by JAX's collectives and lax.ppermute only.
A program may use at most 128 MiB of HBM per device.

v0:
```python
import jax
import jax.numpy as jnp
from jax import lax
from jax.sharding import PartitionSpec as P

GROUP = 64
NBRS = 2
CAP = 2
EPS = 1e-06


def passed_along(value, axis, steps):
    count = lax.axis_size(axis)
    first, last = (max(0, -steps), min(count, count - steps))
    return lax.ppermute(value, axis, [(source, source + steps) for source in range(first, last)])


def rms_scale(values, gain):
    mean_square = jnp.mean(values * values, axis=-1, keepdims=True)
    return values * lax.rsqrt(mean_square + EPS) * gain


def attend(query_blocks, key_blocks, value_blocks):
    scale = query_blocks.shape[-1] ** (-0.5)
    scores = (
        jnp.einsum("bqhs,bkhs->bhqk", query_blocks, key_blocks, preferred_element_type=jnp.float32)
        * scale
    )
    probs = jax.nn.softmax(scores, axis=-1).astype(jnp.bfloat16)
    return jnp.einsum("bhqk,bkhs->bqhs", probs, value_blocks, preferred_element_type=jnp.float32)


def on_device(corpus, enc_qkv, enc_out, cca_kv, gain_in, gain_out, queries, nbr_ids):
    corp_rows, row_tokens, model_width = corpus.shape
    heads_here = enc_qkv.shape[1]
    head_size = enc_qkv.shape[3]
    row_total = corp_rows * row_tokens
    corpus_flat = corpus.reshape(row_total, model_width)
    normed_in = rms_scale(corpus_flat.astype(jnp.float32), gain_in).astype(jnp.bfloat16)
    projected = jnp.dot(
        normed_in,
        enc_qkv.reshape(model_width, heads_here * 3 * head_size),
        preferred_element_type=jnp.float32,
    )
    projected = projected.astype(jnp.bfloat16).reshape(
        corp_rows, row_tokens, heads_here, 3, head_size
    )
    attended = attend(projected[:, :, :, 0], projected[:, :, :, 1], projected[:, :, :, 2]).astype(
        jnp.bfloat16
    )
    attended = attended.reshape(row_total, heads_here * head_size)
    out_weight = enc_out.reshape(heads_here * head_size, model_width)
    partial_terms = jnp.dot(attended, out_weight, preferred_element_type=jnp.float32)
    enc_sum = lax.psum(partial_terms, "head")
    normed = rms_scale(corpus_flat.astype(jnp.float32) + enc_sum, gain_out).astype(jnp.bfloat16)
    memory_cols = heads_here * 2 * head_size
    shard_piece = lax.all_gather(cca_kv, "seq", axis=0, tiled=True)
    memory = jnp.dot(
        normed,
        shard_piece.reshape(shard_piece.shape[0], memory_cols),
        preferred_element_type=jnp.float32,
    )
    memory = memory.astype(jnp.bfloat16).reshape(corp_rows, row_tokens, heads_here, 2, head_size)
    request_ids = nbr_ids.reshape(-1)
    demand = request_ids.shape[0]
    owners = request_ids // corp_rows
    local_row = request_ids % corp_rows
    request_order = jnp.arange(demand)
    earlier = request_order[None, :] < request_order[:, None]
    same_owner = owners[:, None] == owners[None, :]
    slot_rank = jnp.sum(jnp.logical_and(same_owner, earlier), axis=1)
    slot_index = owners * CAP + slot_rank
    devices = lax.axis_size("seq")
    positions = jnp.arange(devices * CAP)
    matched = positions[:, None] == slot_index[None, :]
    wanted = jnp.sum(jnp.where(matched, local_row[None, :], 0), axis=1).reshape(devices, CAP)
    picked = jnp.take(
        memory, lax.all_to_all(wanted, "seq", split_axis=0, concat_axis=0, tiled=True), axis=0
    )
    fetched = lax.all_to_all(picked, "seq", split_axis=0, concat_axis=0, tiled=True)
    fetched = fetched.reshape(devices * CAP, row_tokens, heads_here, 2, head_size)
    group_memory = jnp.take(fetched, slot_index, axis=0)
    groups_here = nbr_ids.shape[0]
    group_memory = group_memory.reshape(groups_here, NBRS * row_tokens, heads_here, 2, head_size)
    token_count = queries.shape[0]
    lead = GROUP - 1
    before = passed_along(group_memory[groups_here - 1 :], "seq", 1)
    window_memory = jnp.concatenate([before, group_memory], axis=0)
    padded_queries = jnp.concatenate(
        [
            jnp.zeros((1, heads_here, head_size), jnp.bfloat16),
            queries,
            jnp.zeros((lead, heads_here, head_size), jnp.bfloat16),
        ],
        axis=0,
    ).reshape(groups_here + 1, GROUP, heads_here, head_size)
    extended = attend(padded_queries, window_memory[:, :, :, 0], window_memory[:, :, :, 1])
    extended = extended.reshape((groups_here + 1) * GROUP, heads_here, head_size)
    result = extended[1 : 1 + token_count].astype(jnp.bfloat16)
    return result


def solution(mesh):
    placed = (
        P("seq", None, None),
        P(None, "head", None, None),
        P("head", None, None),
        P("seq", "head", None, None),
        P(),
        P(),
        P("seq", "head", None),
        P("seq", None),
    )
    return jax.shard_map(
        on_device, mesh=mesh, in_specs=placed, out_specs=P("seq", "head", None), check_vma=False
    )
```

profile of v0, /device:TPU:104, one launch (start us, length us, event | category | flops | bytes accessed | tf_op | source)
XLA Modules:
  0.0 442.4 jit_solution(8818635364731222058)
XLA Ops:
  7.4 16.4 %copy.108 = bf16[4096,2,3,128]{0,3,2,1:T(8,128)(2,1)} copy(bf16[4096,2,3,128]{3,1,2,0:T(2,128)(2,1)} %param.9) | data formatting | bytes 12582912 | tf_op args[1]
  23.8 3.2 multiply_reduce_fusion.1
  27.2 1.7 multiply_convert_fusion.1
  28.9 1.1 copy-done.3
  30.0 3.5 convolution_convert_fusion
  33.5 1.2 copy.109
  34.6 1.7 reshape.286
  38.5 1.3 fusion.19
  39.9 4.5 %fusion.22 = f32[512,4096]{1,0:T(8,128)} fusion(bf16[256,4096]{1,0:T(8,128)(2,1)S(1)} %bitcast.79, bf16[64,8,2,128]{3,2,1,0:T(2,128)(2,1)S(1)} %bitcast.85), kind=kOutput, calls=%fused_computation.38 | convolution fusion | flops 1073741824 | bytes 10747904 | tf_op jit(solution)/shard_map/dot_general | solution.py:53
  45.7 16.9 %all_to_all.20 = s32[32,1,2]{2,1,0:T(1,128)S(1)} all-to-all(s32[32,1,2]{2,1,0:T(1,128)S(1)} %bitcast.88), channel_id=1, replica_groups=mesh['seq'=32,'head'=8] {'seq'}, dimensions={0} | all-to-all | bytes 512 | tf_op jit(solution)/shard_map/all_to_all | solution.py:78
  63.0 90.3 %all-reduce.2.cloned.1.call-done = f32[512,4096]{1,0:T(8,128)} async-done(((f32[512,4096]{1,0:T(8,128)}), f32[512,4096]{1,0:T(8,128)}) %all-reduce.2.cloned.1.call-update) | async-done | bytes 8388624 | tf_op jit(solution)/shard_map/psum | solution.py:54
  153.3 8.9 %multiply_reduce_fusion = (f32[512]{0:T(512)S(1)}, f32[512,4096]{1,0:T(8,128)}) fusion(f32[512,4096]{1,0:T(8,128)} %all-reduce.2.cloned.1.call-done, bf16[4,128,4096]{2,1,0:T(8,128)(2,1)} %param.8), kind=kLoop, calls=%fused_computation.7 | loop fusion | flops 8388096 | bytes 20973568 | tf_op jit(solution)/shard_map/reduce_sum | solution.py:19
  162.2 7.2 %reshape.289 = bf16[4096,512]{1,0:T(8,128)(2,1)} reshape(bf16[4096,2,2,128]{3,2,1,0:T(2,128)(2,1)} %all-gather.2.cloned.1.call-done) | data formatting | bytes 8388608 | tf_op jit(solution)/shard_map/reshape | solution.py:60
  169.4 6.9 %fusion.7 = bf16[512,512]{1,0:T(8,128)(2,1)S(1)} fusion(bf16[4096,512]{1,0:T(8,128)(2,1)} %reshape.289, f32[512,4096]{1,0:T(8,128)} %get-tuple-element.8, f32[4096]{0:T(1024)S(1)} %copy-done.7, f32[512]{0:T(512)S(1)} %add_rsqrt_fusion), kind=kOutput, calls=%fused_computation.20 | convolution fusion | flops 2154037248 | bytes 13125632 | tf_op jit(solution)/shard_map/dot_general | solution.py:58
  176.5 18.3 %gather_fusion = bf16[64,128,2,2,128]{4,3,2,1,0:T(2,128)(2,1)} fusion(bf16[4,128,2,2,128]{4,3,2,1,0:T(2,128)(2,1)S(1)} %reshape.290, s32[1024]{0:T(1024)S(1)} %pad_clamp_fusion.1), kind=kCustom, calls=%fused_computation | custom fusion | bytes 16777472 | tf_op jit(solution)/shard_map/jit(_take)/gather | solution.py:77
  194.8 7.7 %copy_select_fusion = bf16[32,2,128,2,2,128]{5,2,4,3,1,0:T(8,128)(2,1)} fusion(bf16[32,2,128,2,2,128]{5,4,3,2,1,0:T(2,128)(2,1)} %bitcast.80, pred[32,2]{1,0:T(8,128)(4,1)S(1)} %copy.107), kind=kLoop, calls=%fused_computation.5 | loop fusion | flops 4194304 | bytes 16777280 | tf_op jit(solution)/shard_map/jit(_take)/select_n | solution.py:77
  202.6 10.0 %all-to-all-start.1 = ((bf16[32,2,128,2,2,128]{5,2,4,3,1,0:T(8,128)(2,1)}), bf16[32,2,128,2,2,128]{5,2,4,3,1,0:T(8,128)(2,1)}, u32[]{:S(2)}, u32[]{:S(2)}) async-start(bf16[32,2,128,2,2,128]{5,2,4,3,1,0:T(8,128)(2,1)} %copy_select_fusion), calls=%async_computation.1 | async-start | bytes 16777216 | tf_op jit(solution)/shard_map/all_to_all | solution.py:80
  213.4 198.6 %all-to-all-done.1 = bf16[32,2,128,2,2,128]{5,2,4,3,1,0:T(8,128)(2,1)} async-done(((bf16[32,2,128,2,2,128]{5,2,4,3,1,0:T(8,128)(2,1)}), bf16[32,2,128,2,2,128]{5,2,4,3,1,0:T(8,128)(2,1)}, u32[]{:S(2)}, u32[]{:S(2)}) %all-to-all-start.1) | async-done | bytes 8388640 | tf_op jit(solution)/shard_map/all_to_all | solution.py:80
  412.0 4.3 gather_fusion.1
  416.6 1.9 collective-permute-start
  418.5 1.6 copy_select_fusion.1
  420.1 8.8 %collective-permute-done = bf16[1,256,2,2,128]{4,1,2,0,3:T(8,128)(2,1)S(1)} collective-permute-done((bf16[1,256,2,2,128]{4,1,2,0,3:T(8,128)(2,1)S(1)}, bf16[1,256,2,2,128]{4,1,2,0,3:T(8,128)(2,1)S(1)}, u32[]{:S(2)}, u32[]{:S(2)}) %collective-permute-start) | collective-permute-done | bytes 262176 | tf_op jit(solution)/shard_map/ppermute | solution.py:15
  428.8 3.1 fusion.56
  431.9 2.0 fusion.16
  (62 shorter events, 6.3 us)
Async XLA Ops:
  7.4 32.6 %copy-start = (bf16[2,128,4096]{2,1,0:T(8,128)(2,1)S(1)}, bf16[2,128,4096]{2,1,0:T(8,128)(2,1)}, u32[]{:S(2)}) copy-start(bf16[2,128,4096]{2,1,0:T(8,128)(2,1)} %param.10) | copy-start | bytes 6291460
  7.4 145.9 %all-reduce.2.cloned.1.call-start = ((), (), s32[]{:S(2)}) async-start(), calls=%async_computation.2 | async-start | bytes 16777216 | tf_op jit(solution)/shard_map/psum | solution.py:54
  7.4 19.6 %copy-start.5 = (f32[4096]{0:T(1024)S(1)}, f32[4096]{0:T(1024)}, u32[]{:S(2)}) copy-start(f32[4096]{0:T(1024)} %param.12) | copy-start | bytes 49156
  23.8 3.4 copy-start.2
  27.2 2.8 copy-start.3
  44.4 0.7 copy-start.6
  44.4 117.7 %all-gather.2.cloned.1.call-start = ((), (), s32[]{:S(2)}) async-start(), calls=%async_computation.3 | async-start | bytes 4325376 | tf_op jit(solution)/shard_map/all_gather | solution.py:57
  162.1 7.3 %copy-start.7 = (f32[4096]{0:T(1024)S(1)}, f32[4096]{0:T(1024)}, u32[]{:S(2)}) copy-start(f32[4096]{0:T(1024)} %param.13) | copy-start | bytes 49156
  202.6 10.3 %copy-start.4 = (bf16[512,2,128]{2,1,0:T(2,128)(2,1)S(1)}, bf16[512,2,128]{2,1,0:T(2,128)(2,1)}, u32[]{:S(2)}) copy-start(bf16[512,2,128]{2,1,0:T(2,128)(2,1)} %param.14) | copy-start | bytes 786436
  202.6 209.4 %all-to-all-start.1 = ((bf16[32,2,128,2,2,128]{5,2,4,3,1,0:T(8,128)(2,1)}), bf16[32,2,128,2,2,128]{5,2,4,3,1,0:T(8,128)(2,1)}, u32[]{:S(2)}, u32[]{:S(2)}) async-start(bf16[32,2,128,2,2,128]{5,2,4,3,1,0:T(8,128)(2,1)} %copy_select_fusion), calls=%async_computation.1 | async-start | bytes 16777216 | tf_op jit(solution)/shard_map/all_to_all | solution.py:80
  416.6 12.3 %collective-permute-start = (bf16[1,256,2,2,128]{4,1,2,0,3:T(8,128)(2,1)S(1)}, bf16[1,256,2,2,128]{4,1,2,0,3:T(8,128)(2,1)S(1)}, u32[]{:S(2)}, u32[]{:S(2)}) collective-permute-start(bf16[1,256,2,2,128]{4,1,2,0,3:T(8,128)(2,1)S(1)} %bitcast.87), channel_id=1, source_target_pairs={{0,8},{8,16},{16,24},{24,32},{32,40},{40,48},{48,56},{56,64},{64,7... | collective-permute-start | bytes 786440 | tf_op jit(solution)/shard_map/ppermute | solution.py:15
  428.8 6.1 %copy-start.1 = (bf16[2,128,4096]{2,1,0:T(8,128)(2,1)S(1)}, bf16[2,128,4096]{2,1,0:T(8,128)(2,1)}, u32[]{:S(2)}) copy-start(bf16[2,128,4096]{2,1,0:T(8,128)(2,1)} %param.10) | copy-start | bytes 6291460
Sparse Core Ops, SparseCore 0:
  44.6 108.6 all-reduce.1
Sparse Core Ops, SparseCore 1:
  47.5 83.2 all-gather.1
where the time goes:
time: 443 us; the launch traced here: 442 us
  waiting for transfers between devices  298 us (67%)
  local copies, waits for them, and re-layouts  54.6 us (12%)
  other arithmetic  23.7 us (5%)
  matrix products  21.9 us (5%)
  blocking collectives  16.9 us (4%)
  between operations  15.1 us (3%)
  starting transfers between devices  12 us (3%)
    all_to_all x1, waiting for transfers between devices, on_device(): lax.all_to_all(picked, 'seq', split_axis=0, concat_axis=0, tiled=True)  199 us
    psum x1, waiting for transfers between devices, on_device(): enc_sum = lax.psum(partial_terms, 'head')  90.3 us
    unnamed x21, local copies, waits for them, and re-layouts  18.3 us
    gather x1, local copies, waits for them, and re-layouts, on_device(): jnp.take(memory, lax.all_to_all(wanted, 'seq', split_axis=0, concat_axis=...  18.3 us
    all_to_all x1, blocking collectives, on_device(): lax.all_to_all(wanted, 'seq', split_axis=0, concat_axis=0, tiled=True)  16.9 us
    reduce_sum x2, other arithmetic, rms_scale(): mean_square = jnp.mean(values * values, axis=-1, keepdims=True)  12.1 us
    all_to_all x1, starting transfers between devices, on_device(): lax.all_to_all(picked, 'seq', split_axis=0, concat_axis=0, tiled=True)  10 us
  transfers between devices with their start and end apart: 4, of which 3 were waited for; matrix products, arithmetic and copies ran while one was open for 3% of the time, Pallas kernels for 0%

commit v1 on v0

--- a/solution.py
+++ b/solution.py
@@ -7,6 +7,15 @@
 NBRS = 2
 CAP = 2
 EPS = 1e-06
+
+
+def add_in_pairs(array, axis):
+    count = lax.axis_size(axis)
+    total, far = (array, 1)
+    while far < count:
+        total = total + lax.ppermute(total, axis, [(i, i ^ far) for i in range(count)])
+        far = 2 * far
+    return total
 
 
 def passed_along(value, axis, steps):
@@ -51,7 +60,7 @@
     attended = attended.reshape(row_total, heads_here * head_size)
     out_weight = enc_out.reshape(heads_here * head_size, model_width)
     partial_terms = jnp.dot(attended, out_weight, preferred_element_type=jnp.float32)
-    enc_sum = lax.psum(partial_terms, "head")
+    enc_sum = add_in_pairs(partial_terms, "head")
     normed = rms_scale(corpus_flat.astype(jnp.float32) + enc_sum, gain_out).astype(jnp.bfloat16)
     memory_cols = heads_here * 2 * head_size
     shard_piece = lax.all_gather(cca_kv, "seq", axis=0, tiled=True)

time: 443 us -> 709 us (1.60); the launches traced: 442 us -> 701 us
  waiting for transfers between devices: 298 us -> 536 us
  other arithmetic: 23.7 us -> 45.3 us
  matrix products: 21.9 us -> 14 us
    ppermute x0 -> x3, waiting for transfers between devices: none -> 287 us  [add_in_pairs(): lax.ppermute(total, axis, [(i, i ^ far) for i in range(count)])]
    psum x1 -> x0, waiting for transfers between devices: 90.3 us -> none  [on_device(): enc_sum = lax.psum(partial_terms, 'head')]
    all_gather x1, waiting for transfers between devices: 0.02 us -> 64.4 us  [on_device(): shard_piece = lax.all_gather(cca_kv, 'seq', axis=0, tiled=True)]
    add x0 -> x2, other arithmetic: none -> 22.2 us  [add_in_pairs(): total + lax.ppermute(total, axis, [(i, i ^ far) for i in range(count)])]
    all_to_all x1, waiting for transfers between devices: 199 us -> 179 us  [on_device(): lax.all_to_all(picked, 'seq', split_axis=0, concat_axis=0, tiled=True)]
    unnamed x21 -> x25, local copies, waits for them, and re-layouts: 18.3 us -> 21.5 us
  transfers between devices with their start and end apart: 4 -> 6, of which waited for: 3 -> 6; matrix products, arithmetic and copies ran while one was open for 3% -> 1% of each run, Pallas kernels for 0% -> 0%
where the time goes in v1:
time: 709 us; the launch traced here: 701 us
  waiting for transfers between devices  536 us (76%)
  local copies, waits for them, and re-layouts  57.8 us (8%)
  other arithmetic  45.3 us (6%)
  blocking collectives  16.9 us (2%)
  starting transfers between devices  16.5 us (2%)
  matrix products  14 us (2%)
  between operations  13.7 us (2%)
    ppermute x3, waiting for transfers between devices, add_in_pairs(): lax.ppermute(total, axis, [(i, i ^ far) for i in range(count)])  287 us
    all_to_all x1, waiting for transfers between devices, on_device(): lax.all_to_all(picked, 'seq', split_axis=0, concat_axis=0, tiled=True)  179 us
    all_gather x1, waiting for transfers between devices, on_device(): shard_piece = lax.all_gather(cca_kv, 'seq', axis=0, tiled=True)  64.4 us
    add x2, other arithmetic, add_in_pairs(): total + lax.ppermute(total, axis, [(i, i ^ far) for i in range(count)])  22.2 us
    unnamed x25, local copies, waits for them, and re-layouts  21.5 us
    gather x1, local copies, waits for them, and re-layouts, on_device(): jnp.take(memory, lax.all_to_all(wanted, 'seq', split_axis=0, concat_axis=...  18.3 us
    all_to_all x1, blocking collectives, on_device(): lax.all_to_all(wanted, 'seq', split_axis=0, concat_axis=0, tiled=True)  16.9 us
  transfers between devices with their start and end apart: 6, of which 6 were waited for; matrix products, arithmetic and copies ran while one was open for 1% of the time, Pallas kernels for 0%

profile of v1, /device:TPU:104, one launch (start us, length us, event | category | flops | bytes accessed | tf_op | source)
XLA Modules:
  0.0 700.5 jit_solution(12309918819749419952)
XLA Ops:
  6.5 16.4 %copy.108 = bf16[4096,2,3,128]{0,3,2,1:T(8,128)(2,1)} copy(bf16[4096,2,3,128]{3,1,2,0:T(2,128)(2,1)} %param.9) | data formatting | bytes 12582912 | tf_op args[1]
  22.9 3.2 multiply_reduce_fusion.1
  29.2 3.5 convolution_convert_fusion
  40.4 3.2 copy-done.3
  43.6 13.3 %collective-permute-done = f32[512,4096]{1,0:T(8,128)} collective-permute-done((f32[512,4096]{1,0:T(8,128)S(1)}, f32[512,4096]{1,0:T(8,128)}, u32[]{:S(2)}, u32[]{:S(2)}) %collective-permute-start) | collective-permute-done | bytes 8388640 | tf_op jit(solution)/shard_map/ppermute | solution.py:16
  56.9 11.1 %add.125 = f32[512,4096]{1,0:T(8,128)} add(f32[512,4096]{1,0:T(8,128)} %copy-done.3, f32[512,4096]{1,0:T(8,128)} %collective-permute-done) | non-fusion elementwise | flops 2097152 | bytes 25165824 | tf_op jit(solution)/shard_map/add | solution.py:16
  68.4 182.4 %collective-permute-done.1 = f32[512,4096]{1,0:T(8,128)} collective-permute-done((f32[512,4096]{1,0:T(8,128)}, f32[512,4096]{1,0:T(8,128)}, u32[]{:S(2)}, u32[]{:S(2)}) %collective-permute-start.1) | collective-permute-done | bytes 8388640 | tf_op jit(solution)/shard_map/ppermute | solution.py:16
  250.8 11.1 %add.126 = f32[512,4096]{1,0:T(8,128)} add(f32[512,4096]{1,0:T(8,128)} %add.125, f32[512,4096]{1,0:T(8,128)} %collective-permute-done.1) | non-fusion elementwise | flops 2097152 | bytes 25165824 | tf_op jit(solution)/shard_map/add | solution.py:16
  261.9 2.3 collective-permute-start.2
  264.8 16.9 %all_to_all.20 = s32[32,1,2]{2,1,0:T(1,128)S(1)} all-to-all(s32[32,1,2]{2,1,0:T(1,128)S(1)} %bitcast.88), channel_id=1, replica_groups=mesh['seq'=32,'head'=8] {'seq'}, dimensions={0} | all-to-all | bytes 512 | tf_op jit(solution)/shard_map/all_to_all | solution.py:87
  282.2 64.4 %all-gather.2.cloned.1.call-done = bf16[4096,2,2,128]{3,2,1,0:T(2,128)(2,1)} async-done(((bf16[128,2,2,128]{3,2,1,0:T(2,128)(2,1)}), bf16[4096,2,2,128]{3,2,1,0:T(2,128)(2,1)}) %all-gather.2.cloned.1.call-update) | async-done | bytes 4194320 | tf_op jit(solution)/shard_map/all_gather | solution.py:66
  346.6 7.2 %reshape.289 = bf16[4096,512]{1,0:T(8,128)(2,1)} reshape(bf16[4096,2,2,128]{3,2,1,0:T(2,128)(2,1)} %all-gather.2.cloned.1.call-done) | data formatting | bytes 8388608 | tf_op jit(solution)/shard_map/reshape | solution.py:69
  353.8 91.6 %collective-permute-done.2 = f32[512,4096]{1,0:T(8,128)} collective-permute-done((f32[512,4096]{1,0:T(8,128)}, f32[512,4096]{1,0:T(8,128)}, u32[]{:S(2)}, u32[]{:S(2)}) %collective-permute-start.2) | collective-permute-done | bytes 8388640 | tf_op jit(solution)/shard_map/ppermute | solution.py:16
  445.4 8.1 %multiply_reduce_fusion = (f32[512]{0:T(512)S(1)}, f32[512,4096]{1,0:T(8,128)S(1)}) fusion(f32[512,4096]{1,0:T(8,128)} %add.126, f32[512,4096]{1,0:T(8,128)} %collective-permute-done.2, bf16[4,128,4096]{2,1,0:T(8,128)(2,1)} %param.8), kind=kLoop, calls=%fused_computation.7 | loop fusion | flops 10485248 | bytes 29362176 | tf_op jit(solution)/shard_map/reduce_sum | solution.py:28
  453.6 2.4 fusion.7
  456.1 18.3 %gather_fusion = bf16[64,128,2,2,128]{4,3,2,1,0:T(2,128)(2,1)} fusion(bf16[4,128,2,2,128]{4,3,2,1,0:T(2,128)(2,1)S(1)} %reshape.290, s32[1024]{0:T(1024)S(1)} %pad_clamp_fusion.1), kind=kCustom, calls=%fused_computation | custom fusion | bytes 16777472 | tf_op jit(solution)/shard_map/jit(_take)/gather | solution.py:86
  474.4 7.7 %copy_select_fusion = bf16[32,2,128,2,2,128]{5,2,4,3,1,0:T(8,128)(2,1)} fusion(bf16[32,2,128,2,2,128]{5,4,3,2,1,0:T(2,128)(2,1)} %bitcast.80, pred[32,2]{1,0:T(8,128)(4,1)S(1)} %copy.107), kind=kLoop, calls=%fused_computation.5 | loop fusion | flops 4194304 | bytes 16777280 | tf_op jit(solution)/shard_map/jit(_take)/select_n | solution.py:86
  482.2 10.4 %all-to-all-start.1 = ((bf16[32,2,128,2,2,128]{5,2,4,3,1,0:T(8,128)(2,1)}), bf16[32,2,128,2,2,128]{5,2,4,3,1,0:T(8,128)(2,1)}, u32[]{:S(2)}, u32[]{:S(2)}) async-start(bf16[32,2,128,2,2,128]{5,2,4,3,1,0:T(8,128)(2,1)} %copy_select_fusion), calls=%async_computation.1 | async-start | bytes 16777216 | tf_op jit(solution)/shard_map/all_to_all | solution.py:89
  493.4 179.1 %all-to-all-done.1 = bf16[32,2,128,2,2,128]{5,2,4,3,1,0:T(8,128)(2,1)} async-done(((bf16[32,2,128,2,2,128]{5,2,4,3,1,0:T(8,128)(2,1)}), bf16[32,2,128,2,2,128]{5,2,4,3,1,0:T(8,128)(2,1)}, u32[]{:S(2)}, u32[]{:S(2)}) %all-to-all-start.1) | async-done | bytes 8388640 | tf_op jit(solution)/shard_map/all_to_all | solution.py:89
  672.6 4.3 gather_fusion.1
  677.2 3.3 collective-permute-start.3
  682.1 5.5 collective-permute-done.3
  687.5 3.1 fusion.56
  690.6 2.0 fusion.16
  (71 shorter events, 15.9 us)
Async XLA Ops:
  6.5 32.5 %copy-start = (bf16[2,128,4096]{2,1,0:T(8,128)(2,1)S(1)}, bf16[2,128,4096]{2,1,0:T(8,128)(2,1)}, u32[]{:S(2)}) copy-start(bf16[2,128,4096]{2,1,0:T(8,128)(2,1)} %param.10) | copy-start | bytes 6291460
  6.5 340.0 %all-gather.2.cloned.1.call-start = ((), (), s32[]{:S(2)}) async-start(), calls=%async_computation.2 | async-start | bytes 4325376 | tf_op jit(solution)/shard_map/all_gather | solution.py:66
  6.5 19.6 %copy-start.7 = (f32[4096]{0:T(1024)S(1)}, f32[4096]{0:T(1024)}, u32[]{:S(2)}) copy-start(f32[4096]{0:T(1024)} %param.12) | copy-start | bytes 49156
  22.9 3.4 copy-start.2
  26.4 2.8 copy-start.4
  40.3 3.2 copy-start.3
  43.6 13.3 %collective-permute-start = (f32[512,4096]{1,0:T(8,128)S(1)}, f32[512,4096]{1,0:T(8,128)}, u32[]{:S(2)}, u32[]{:S(2)}) collective-permute-start(f32[512,4096]{1,0:T(8,128)S(1)} %fusion.22), channel_id=1, source_target_pairs={{0,1},{1,0},{2,3},{3,2},{4,5},{5,4},{6,7},{7,6},{8,9},{9,8},{10,11... | collective-permute-start | bytes 25165832 | tf_op jit(solution)/shard_map/ppermute | solution.py:16
  68.0 196.3 %copy-start.8 = (s32[8,2]{0,1:T(2,128)S(1)}, s32[8,2]{0,1:T(2,128)}, u32[]{:S(2)}) copy-start(s32[8,2]{0,1:T(2,128)} %param.15) | copy-start | bytes 196
  68.0 182.8 %collective-permute-start.1 = (f32[512,4096]{1,0:T(8,128)}, f32[512,4096]{1,0:T(8,128)}, u32[]{:S(2)}, u32[]{:S(2)}) collective-permute-start(f32[512,4096]{1,0:T(8,128)} %add.125), channel_id=1, source_target_pairs={{0,2},{1,3},{2,0},{3,1},{4,6},{5,7},{6,4},{7,5},{8,10},{9,11},{10,... | collective-permute-start | bytes 25165832 | tf_op jit(solution)/shard_map/ppermute | solution.py:16
  261.9 183.5 %collective-permute-start.2 = (f32[512,4096]{1,0:T(8,128)}, f32[512,4096]{1,0:T(8,128)}, u32[]{:S(2)}, u32[]{:S(2)}) collective-permute-start(f32[512,4096]{1,0:T(8,128)} %add.126), channel_id=1, source_target_pairs={{0,4},{1,5},{2,6},{3,7},{4,0},{5,1},{6,2},{7,3},{8,12},{9,13},{10,... | collective-permute-start | bytes 25165832 | tf_op jit(solution)/shard_map/ppermute | solution.py:16
  353.8 99.8 %copy-start.5 = (bf16[4096,512]{1,0:T(8,128)(2,1)S(1)}, bf16[4096,512]{1,0:T(8,128)(2,1)}, u32[]{:S(2)}) copy-start(bf16[4096,512]{1,0:T(8,128)(2,1)} %reshape.289) | copy-start | bytes 12582916
  353.8 99.8 %copy-start.9 = (f32[4096]{0:T(1024)S(1)}, f32[4096]{0:T(1024)}, u32[]{:S(2)}) copy-start(f32[4096]{0:T(1024)} %param.13) | copy-start | bytes 49156
  482.2 10.8 %copy-start.6 = (bf16[512,2,128]{2,1,0:T(2,128)(2,1)S(1)}, bf16[512,2,128]{2,1,0:T(2,128)(2,1)}, u32[]{:S(2)}) copy-start(bf16[512,2,128]{2,1,0:T(2,128)(2,1)} %param.14) | copy-start | bytes 786436
  482.2 190.4 %all-to-all-start.1 = ((bf16[32,2,128,2,2,128]{5,2,4,3,1,0:T(8,128)(2,1)}), bf16[32,2,128,2,2,128]{5,2,4,3,1,0:T(8,128)(2,1)}, u32[]{:S(2)}, u32[]{:S(2)}) async-start(bf16[32,2,128,2,2,128]{5,2,4,3,1,0:T(8,128)(2,1)} %copy_select_fusion), calls=%async_computation.1 | async-start | bytes 16777216 | tf_op jit(solution)/shard_map/all_to_all | solution.py:89
  677.2 10.4 %collective-permute-start.3 = (bf16[1,256,2,2,128]{4,1,2,0,3:T(8,128)(2,1)S(1)}, bf16[1,256,2,2,128]{4,1,2,0,3:T(8,128)(2,1)S(1)}, u32[]{:S(2)}, u32[]{:S(2)}) collective-permute-start(bf16[1,256,2,2,128]{4,1,2,0,3:T(8,128)(2,1)S(1)} %bitcast.87), channel_id=1, source_target_pairs={{0,8},{8,16},{16,24},{24,32},{32,40},{40,48},{48,56},{56,64},{64,7... | collective-permute-start | bytes 786440 | tf_op jit(solution)/shard_map/ppermute | solution.py:24
  687.5 6.1 copy-start.1
Sparse Core Ops, SparseCore 0:
  264.4 82.1 all-gather.1
